TPU v7x, 256 devices: a whole 4x4x8 slice. The times are simulated.
256 devices in a mesh: row: 8 (over x, y_lo), col: 32 (over y_hi, z, core).
Axes of the slice: x: 4, y: 4 (y_hi: 2, y_lo: 2; y = y_hi * 2 + y_lo), z: 8, core: 2. Of those that a mesh axis runs over, the one named last changes fastest.
Arguments:
- features: bfloat16 [65536, 128], P(('row', 'col')), may hold values from -6 to 6
- degrees: int32 [65536], P(('row', 'col')), may hold values from 32 to 159
- adj_tiles: bfloat16 [8, 32, 256, 4096], P('row', 'col'), may hold values from 0 to 0.22472483, as said below
- tile_rows: int32 [8, 32, 256], P('row', 'col'), may hold values from 0 to 127
- tile_cols: int32 [8, 32, 256], P('row', 'col'), may hold values from 0 to 31
- tile_counts: int32 [8, 32], P('row', 'col'), may hold values from 64 to 256, as said below
Outputs:
- propagated: bfloat16 [65536, 128], P(('row', 'col'))
Inputs may be any that keep to these rules, and one draw needn't show every extreme that they name: Each block holds at most 256 live tiles, in its first tile_counts slots; some block holds exactly 256. `adj_tiles`: edge weights are zero or positive.
All inputs are finite; a program needn't handle non-finite values.
Results may differ from a plain program's by a relative error of at most 0.0054.
Values may be sent and summed in bfloat16 or wider, within the bound.
A program may use at most 128 MiB of HBM per device.

v0:
```python
import jax
import jax.numpy as jnp
from jax import lax
from jax.sharding import PartitionSpec as P

TILE = 64
KNN = 32
STEPS = 2
ALPHA = 0.1


def shards(features, degrees, adj_tiles, tile_rows, tile_cols, tile_counts):
    col_count = lax.axis_size("col")
    nodes_dev = features.shape[0]
    feat_width = features.shape[1]
    tile_slots = adj_tiles.shape[2]
    dev_tiles = adj_tiles.reshape(tile_slots, TILE, TILE)
    row_ids_all = tile_rows.reshape(tile_slots)
    col_ids_all = tile_cols.reshape(tile_slots)
    live_count = tile_counts.reshape(())
    block_len = min(256, tile_slots)
    num_turns = tile_slots // block_len
    row_tiles = nodes_dev * col_count // TILE
    norm_scale = jnp.sqrt(KNN / degrees.astype(jnp.float32))[:, None]
    teleport = ALPHA * features.astype(jnp.float32)
    current = features.astype(jnp.float32)
    for repeat in range(STEPS):
        source = (norm_scale * current).astype(jnp.bfloat16)
        col_panel = lax.all_gather(source, "row", axis=0, tiled=True).reshape(-1, TILE, feat_width)

        def add_block(turn_index, totals):
            first_tile = turn_index * block_len
            live_mask = first_tile + jnp.arange(block_len, dtype=jnp.int32) < live_count
            inputs = col_panel[col_ids_all]
            products = jnp.einsum(
                "tab,tbf->taf", dev_tiles, inputs, preferred_element_type=jnp.float32
            )
            products = jnp.where(live_mask[:, None, None], products, jnp.zeros_like(products))
            return totals.at[row_ids_all].add(products)

        start_tot = jnp.zeros((row_tiles, TILE, feat_width), jnp.float32)
        totals = lax.fori_loop(0, num_turns, add_block, start_tot)
        partial_rows = totals.reshape(row_tiles * TILE, feat_width)
        summed = lax.psum(partial_rows, "col")
        own_rows = lax.dynamic_slice_in_dim(summed, lax.axis_index("col") * nodes_dev, nodes_dev, 0)
        current = (1.0 - ALPHA) * norm_scale * own_rows + teleport
    return current.astype(jnp.bfloat16)


def solution(mesh):
    return jax.shard_map(
        shards,
        mesh=mesh,
        in_specs=(
            P(("row", "col"), None),
            P(("row", "col")),
            P("row", "col", None, None),
            P("row", "col", None),
            P("row", "col", None),
            P("row", "col"),
        ),
        out_specs=P(("row", "col"), None),
        check_vma=False,
    )
```

profile of v0, /device:TPU:1, one launch (start us, length us, event | category | flops | bytes accessed | tf_op | source)
XLA Modules:
  0.0 748.5 jit_solution(6147863713044268704)
XLA Ops:
  6.5 0.0 all-reduce.3.cloned.1.call-start
  7.2 0.7 compare_select_fusion.1
  7.9 0.7 compare_select_fusion
  8.6 0.7 broadcast_multiply_fusion
  9.3 0.9 fusion.5
  10.2 24.6 %all_gather.6 = bf16[2048,128]{1,0:T(8,128)(2,1)S(1)} all-gather(bf16[256,128]{1,0:T(8,128)(2,1)S(1)} %fusion.5), channel_id=1, replica_groups=mesh['row'=8,'col'=32] {'row'}, dimensions={0}, use_global_device_ids=true | all-gather | bytes 589824 | tf_op jit(solution)/shard_map/all_gather | solution.py:29
  34.8 3.3 copy.7
  38.1 6.6 copy.8
  44.8 3.0 gather_fusion
  47.8 7.9 %select_bitcast_fusion.1 = f32[256,64,128]{2,1,0:T(8,128)} fusion(pred[256]{0:T(512)(128)(4,1)S(1)} %iota_compare_fusion, bf16[256,64,64]{2,1,0:T(8,128)(2,1)} %copy.8, bf16[256,64,128]{2,1,0:T(8,128)(2,1)} %gather_fusion), kind=kOutput, calls=%fused_computation.5 | convolution fusion | flops 270532608 | bytes 14680320 | tf_op jit(solution)/shard_map/while/body/eval_jaxpr/tab,tbf->taf/dot_general | solution.py:35
  55.7 2.5 broadcast.71.clone
  58.2 39.4 %scatter_fusion = f32[128,64,128]{2,1,0:T(8,128)} fusion(f32[128,64,128]{2,1,0:T(8,128)} %broadcast.71.clone, s32[256]{0:T(256)S(1)} %bitcast.26, f32[256,64,128]{2,1,0:T(8,128)} %select_bitcast_fusion.1), kind=kCustom, calls=%fused_computation.2 | custom fusion | flops 2097152 | bytes 25166848 | tf_op jit(solution)/shard_map/while/body/eval_jaxpr/scatter-add | solution.py:39
  97.6 0.0 copy-start
  97.6 0.0 all-reduce.3.cloned.1.call-update
  97.6 0.0 all-reduce.5.cloned.1.call-start
  97.7 286.3 %all-reduce.3.cloned.1.call-done = f32[8192,128]{1,0:T(8,128)} async-done(((f32[8192,128]{1,0:T(8,128)}), f32[8192,128]{1,0:T(8,128)}) %all-reduce.3.cloned.1.call-update) | async-done | bytes 4194320 | tf_op jit(solution)/shard_map/psum | solution.py:44
  384.0 0.0 copy-done
  384.0 1.0 fusion.3
  385.0 23.4 %all_gather.7 = bf16[2048,128]{1,0:T(8,128)(2,1)S(1)} all-gather(bf16[256,128]{1,0:T(8,128)(2,1)S(1)} %fusion.3), channel_id=1, replica_groups=mesh['row'=8,'col'=32] {'row'}, dimensions={0}, use_global_device_ids=true | all-gather | bytes 589824 | tf_op jit(solution)/shard_map/all_gather | solution.py:29
  408.4 3.1 gather_fusion.1
  411.5 7.9 %select_bitcast_fusion = f32[256,64,128]{2,1,0:T(8,128)} fusion(pred[256]{0:T(512)(128)(4,1)S(1)} %iota_compare_fusion, bf16[256,64,64]{2,1,0:T(8,128)(2,1)} %copy.8, bf16[256,64,128]{2,1,0:T(8,128)(2,1)} %gather_fusion.1), kind=kOutput, calls=%fused_computation.4 | convolution fusion | flops 270532608 | bytes 14680320 | tf_op jit(solution)/shard_map/while/body/eval_jaxpr/tab,tbf->taf/dot_general | solution.py:35
  419.4 2.5 broadcast.71
  421.9 39.3 %scatter_fusion.1 = f32[128,64,128]{2,1,0:T(8,128)} fusion(f32[128,64,128]{2,1,0:T(8,128)} %broadcast.71, s32[256]{0:T(256)S(1)} %bitcast.27, f32[256,64,128]{2,1,0:T(8,128)} %select_bitcast_fusion), kind=kCustom, calls=%fused_computation.3 | custom fusion | flops 2097152 | bytes 25166848 | tf_op jit(solution)/shard_map/while/body/eval_jaxpr/scatter-add | solution.py:39
  461.2 0.0 all-reduce.5.cloned.1.call-update
  461.3 278.8 %all-reduce.5.cloned.1.call-done = f32[8192,128]{1,0:T(8,128)} async-done(((f32[8192,128]{1,0:T(8,128)}), f32[8192,128]{1,0:T(8,128)}) %all-reduce.5.cloned.1.call-update) | async-done | bytes 4194320 | tf_op jit(solution)/shard_map/psum | solution.py:44
  740.1 1.6 fusion.4
  (2 shorter events, 0.0 us)
Async XLA Ops:
  6.5 377.4 %all-reduce.3.cloned.1.call-start = ((), (), s32[]{:S(2)}) async-start(), calls=%async_computation | async-start | bytes 8388608 | tf_op jit(solution)/shard_map/psum | solution.py:44
  97.6 286.3 %copy-start = (bf16[256,128]{1,0:T(8,128)(2,1)S(1)}, bf16[256,128]{1,0:T(8,128)(2,1)}, u32[]{:S(2)}) copy-start(bf16[256,128]{1,0:T(8,128)(2,1)} %param.6) | copy-start | bytes 196612
  97.6 642.4 %all-reduce.5.cloned.1.call-start = ((), (), s32[]{:S(2)}) async-start(), calls=%async_computation.1 | async-start | bytes 8388608 | tf_op jit(solution)/shard_map/psum | solution.py:44
Sparse Core Ops, SparseCore 0:
  97.8 286.1 all-reduce.2
  461.4 278.6 all-reduce.4
where the time goes:
time: 750 us; the launch traced here: 749 us
  waiting for transfers between devices  565 us (75%)
  other arithmetic  84.4 us (11%)
  blocking collectives  48.1 us (6%)
  local copies, waits for them, and re-layouts  21 us (3%)
  matrix products  15.9 us (2%)
  between operations  14.1 us (2%)
    psum x2, waiting for transfers between devices, shards(): summed = lax.psum(partial_rows, 'col')  565 us
    scatter-add x2, other arithmetic, add_block(): return totals.at[row_ids_all].add(products)  78.7 us
    all_gather x2, blocking collectives, shards(): lax.all_gather(source, 'row', axis=0, tiled=True)  48.1 us
    dot_general x2, matrix products, add_block(): jnp.einsum('tab,tbf->taf', dev_tiles, inputs, preferred_element_type=jnp....  15.9 us
  transfers between devices with their start and end apart: 2, of which 2 were waited for; matrix products, arithmetic and copies ran while one was open for 0% of the time, Pallas kernels for 0%

commit v1 on v0

--- a/solution.py
+++ b/solution.py
@@ -26,7 +26,9 @@
     current = features.astype(jnp.float32)
     for repeat in range(STEPS):
         source = (norm_scale * current).astype(jnp.bfloat16)
-        col_panel = lax.all_gather(source, "row", axis=0, tiled=True).reshape(-1, TILE, feat_width)
+        col_panel = jnp.concatenate(
+            lax.all_to_all(jnp.stack([source] * lax.axis_size("row")), "row", 0, 0), axis=0
+        ).reshape(-1, TILE, feat_width)
 
         def add_block(turn_index, totals):
             first_tile = turn_index * block_len

time: 750 us -> 711 us (0.948)
  blocking collectives: 48.1 us -> 12.4 us
  waiting for transfers between devices: 565 us -> 556 us
    all_gather x2 -> x0, blocking collectives: 48.1 us -> none  [shards(): lax.all_gather(source, 'row', axis=0, tiled=True)]
    all_to_all x0 -> x1, blocking collectives: none -> 12.4 us  [shards(): lax.all_to_all(jnp.stack([source] * lax.axis_size('row')), 'row', 0, 0)]
    psum x2, waiting for transfers between devices: 565 us -> 556 us  [shards(): summed = lax.psum(partial_rows, 'col')]
  transfers between devices with their start and end apart: 2 -> 3, of which waited for: 2 -> 2; matrix products, arithmetic and copies ran while one was open for 0% -> 1% of each run, Pallas kernels for 0% -> 0%
where the time goes in v1:
time: 711 us; the launch traced here: 710 us
  waiting for transfers between devices  556 us (78%)
  other arithmetic  83.7 us (12%)
  local copies, waits for them, and re-layouts  21.9 us (3%)
  matrix products  15.9 us (2%)
  between operations  14.1 us (2%)
  blocking collectives  12.4 us (2%)
    psum x2, waiting for transfers between devices, shards(): summed = lax.psum(partial_rows, 'col')  556 us
    scatter-add x2, other arithmetic, add_block(): return totals.at[row_ids_all].add(products)  78.7 us
    dot_general x2, matrix products, add_block(): jnp.einsum('tab,tbf->taf', dev_tiles, inputs, preferred_element_type=jnp....  15.9 us
  transfers between devices with their start and end apart: 3, of which 2 were waited for; matrix products, arithmetic and copies ran while one was open for 1% of the time, Pallas kernels for 0%

profile of v1, /device:TPU:1, one launch (start us, length us, event | category | flops | bytes accessed | tf_op | source)
XLA Modules:
  0.0 710.3 jit_solution(12768226916152396711)
XLA Ops:
  6.5 0.7 broadcast_multiply_fusion
  7.2 0.9 fusion.5
  8.2 0.9 stack.4
  9.0 5.9 all-to-all-start
  14.9 0.0 all-reduce.3.cloned.1.call-start
  14.9 0.7 compare_select_fusion
  16.3 3.3 copy.7
  19.6 0.0 copy-start.1
  19.6 6.6 copy.8
  26.2 0.0 copy-done.1
  26.2 0.0 all-to-all-done
  26.3 3.1 gather_fusion
  29.3 7.9 %select_bitcast_fusion.1 = f32[256,64,128]{2,1,0:T(8,128)} fusion(pred[256]{0:T(512)(128)(4,1)S(1)} %iota_compare_fusion, bf16[256,64,64]{2,1,0:T(8,128)(2,1)} %copy.8, bf16[256,64,128]{2,1,0:T(8,128)(2,1)} %gather_fusion), kind=kOutput, calls=%fused_computation.5 | convolution fusion | flops 270532608 | bytes 14680320 | tf_op jit(solution)/shard_map/while/body/eval_jaxpr/tab,tbf->taf/dot_general | solution.py:37
  37.2 2.5 broadcast.75.clone
  39.7 39.4 %scatter_fusion = f32[128,64,128]{2,1,0:T(8,128)} fusion(f32[128,64,128]{2,1,0:T(8,128)} %broadcast.75.clone, s32[256]{0:T(256)S(1)} %bitcast.26, f32[256,64,128]{2,1,0:T(8,128)} %select_bitcast_fusion.1), kind=kCustom, calls=%fused_computation.2 | custom fusion | flops 2097152 | bytes 25166848 | tf_op jit(solution)/shard_map/while/body/eval_jaxpr/scatter-add | solution.py:41
  79.1 0.0 copy-start
  79.1 0.0 all-reduce.3.cloned.1.call-update
  79.1 0.0 all-reduce.5.cloned.1.call-start
  79.2 281.8 %all-reduce.3.cloned.1.call-done = f32[8192,128]{1,0:T(8,128)} async-done(((f32[8192,128]{1,0:T(8,128)}), f32[8192,128]{1,0:T(8,128)}) %all-reduce.3.cloned.1.call-update) | async-done | bytes 4194320 | tf_op jit(solution)/shard_map/psum | solution.py:46
  361.0 0.0 copy-done
  361.0 1.0 fusion.3
  362.1 0.1 stack.5
  362.1 12.4 %all_to_all.10 = bf16[8,256,128]{2,1,0:T(8,128)(2,1)S(1)} all-to-all(bf16[8,256,128]{2,1,0:T(8,128)(2,1)S(1)} %stack.5), channel_id=1, replica_groups=mesh['row'=8,'col'=32] {'row'}, dimensions={0} | all-to-all | bytes 1048576 | tf_op jit(solution)/shard_map/all_to_all | solution.py:30
  374.5 3.0 gather_fusion.1
  377.6 7.9 %select_bitcast_fusion = f32[256,64,128]{2,1,0:T(8,128)} fusion(pred[256]{0:T(512)(128)(4,1)S(1)} %iota_compare_fusion, bf16[256,64,64]{2,1,0:T(8,128)(2,1)} %copy.8, bf16[256,64,128]{2,1,0:T(8,128)(2,1)} %gather_fusion.1), kind=kOutput, calls=%fused_computation.4 | convolution fusion | flops 270532608 | bytes 14680320 | tf_op jit(solution)/shard_map/while/body/eval_jaxpr/tab,tbf->taf/dot_general | solution.py:37
  385.5 2.5 broadcast.75
  388.0 39.3 %scatter_fusion.1 = f32[128,64,128]{2,1,0:T(8,128)} fusion(f32[128,64,128]{2,1,0:T(8,128)} %broadcast.75, s32[256]{0:T(256)S(1)} %bitcast.27, f32[256,64,128]{2,1,0:T(8,128)} %select_bitcast_fusion), kind=kCustom, calls=%fused_computation.3 | custom fusion | flops 2097152 | bytes 25166848 | tf_op jit(solution)/shard_map/while/body/eval_jaxpr/scatter-add | solution.py:41
  427.3 0.0 all-reduce.5.cloned.1.call-update
  427.4 274.4 %all-reduce.5.cloned.1.call-done = f32[8192,128]{1,0:T(8,128)} async-done(((f32[8192,128]{1,0:T(8,128)}), f32[8192,128]{1,0:T(8,128)}) %all-reduce.5.cloned.1.call-update) | async-done | bytes 4194320 | tf_op jit(solution)/shard_map/psum | solution.py:46
  701.8 1.6 fusion.4
  (3 shorter events, 0.0 us)
Async XLA Ops:
  9.0 17.2 %all-to-all-start = ((bf16[8,256,128]{2,1,0:T(8,128)(2,1)}), bf16[8,256,128]{2,1,0:T(8,128)(2,1)S(1)}, u32[]{:S(2)}, u32[]{:S(2)}) async-start(bf16[8,256,128]{2,1,0:T(8,128)(2,1)} %stack.4), calls=%async_computation | async-start | bytes 1048576 | tf_op jit(solution)/shard_map/all_to_all | solution.py:30
  14.9 346.1 %all-reduce.3.cloned.1.call-start = ((), (), s32[]{:S(2)}) async-start(), calls=%async_computation.2 | async-start | bytes 8388608 | tf_op jit(solution)/shard_map/psum | solution.py:46
  19.6 6.7 copy-start.1
  79.1 281.9 %copy-start = (bf16[256,128]{1,0:T(8,128)(2,1)S(1)}, bf16[256,128]{1,0:T(8,128)(2,1)}, u32[]{:S(2)}) copy-start(bf16[256,128]{1,0:T(8,128)(2,1)} %param.6) | copy-start | bytes 196612
  79.1 622.7 %all-reduce.5.cloned.1.call-start = ((), (), s32[]{:S(2)}) async-start(), calls=%async_computation.3 | async-start | bytes 8388608 | tf_op jit(solution)/shard_map/psum | solution.py:46
Sparse Core Ops, SparseCore 0:
  79.3 281.7 all-reduce.2
  427.5 274.2 all-reduce.4
